TPU v7x, 128 devices: a whole 4x4x4 slice. The times are simulated.
128 devices in a mesh: region: 16 (over y_lo, z, core), head: 8 (over y_hi, x).
Axes of the slice: x: 4, y: 4 (y_hi: 2, y_lo: 2; y = y_hi * 2 + y_lo), z: 4, core: 2. Of those that a mesh axis runs over, the one named last changes fastest.
Arguments:
- fine_tokens: float32 [73728, 512], P(('region', 'head')), may hold values from -6 to 6
- fine_shift: int32 [1], replicated, may hold values from 1 to 143
- window_counts: int32 [128], P('region'), may hold values from 36 to 144
- fine_qkv: bfloat16 [512, 1536], replicated, may hold values from -4 to 4
- fine_proj: bfloat16 [512, 512], replicated, may hold values from -0.25 to 0.25
- fine_up: bfloat16 [512, 2048], replicated, may hold values from -0.25 to 0.25
- fine_down: bfloat16 [2048, 512], replicated, may hold values from -0.125 to 0.125
- merge_weight: bfloat16 [2048, 1024], replicated, may hold values from -0.125 to 0.125
- coarse_qkv: bfloat16 [1024, 3072], P('region', 'head'), may hold values from -4 to 4
- coarse_proj: bfloat16 [1024, 1024], P('head', 'region'), may hold values from -0.1875 to 0.1875
- coarse_up: bfloat16 [1024, 4096], P('region', 'head'), may hold values from -0.1875 to 0.1875
- coarse_down: bfloat16 [4096, 1024], P('head', 'region'), may hold values from -0.09375 to 0.09375
- expand_weight: bfloat16 [1024, 2048], replicated, may hold values from -0.1875 to 0.1875
- out_weight: bfloat16 [1024, 512], replicated, may hold values from -0.1875 to 0.1875
Outputs:
- fine_result: float32 [73728, 512], P(('region', 'head'))
All inputs are finite; a program needn't handle non-finite values.
Results may differ from a plain program's by a relative error of at most 0.012.
Values may be sent and summed in bfloat16 or wider, within the bound.
No kernel may reach another device: no remote copies, remote signals or barrier semaphores. Data moves between devices by JAX's collectives and lax.ppermute only.
A program may use at most 128 MiB of HBM per device.

v0:
```python
import jax
import jax.numpy as jnp
from jax import lax
from jax.sharding import PartitionSpec as P

C = 512
HD = 64
HF = 8
HC = 16
WIN = 144


def with_halo(value, sides, width):
    edges = {}
    for axis, dim in sides:
        devices, length = (lax.axis_size(axis), value.shape[dim])
        up = [(i, (i + 1) % devices) for i in range(devices)]
        last = lax.slice_in_dim(value, length - width, length, axis=dim)
        initial = lax.slice_in_dim(value, 0, width, axis=dim)
        edges[dim] = (
            lax.ppermute(last, axis, up),
            lax.ppermute(initial, axis, [(b, a) for a, b in up]),
        )
    done = []
    for _, dim in sides:
        low, high = edges[dim]
        around = [(width, width) if d in done else (0, 0) for d in range(value.ndim)]
        value = jnp.concatenate([jnp.pad(low, around), value, jnp.pad(high, around)], axis=dim)
        done.append(dim)
    return value


def from_everyone(value, axis):
    devices = lax.axis_size(axis)
    return lax.all_to_all(
        jnp.broadcast_to(value[None], (devices, *value.shape)), axis, 0, 0, tiled=True
    )


def laid_out(blocks, dim):
    blocks = jnp.moveaxis(blocks, 0, dim)
    shape = blocks.shape
    return blocks.reshape(*shape[:dim], shape[dim] * shape[dim + 1], *shape[dim + 2 :])


def gathered_copies(value, axis, dim):
    blocks = from_everyone(value, axis)
    return laid_out(blocks, dim)


def turned_gather(arrays, axis, dims):
    turned = [jnp.moveaxis(a, dim, 0) for a, dim in zip(arrays, dims)]
    both = jnp.concatenate([t.reshape(len(t), -1) for t in turned], axis=1)
    filled, at, gathered = (lax.all_gather(both, axis, axis=0, tiled=True), 0, [])
    for t, dim in zip(turned, dims):
        share = filled[:, at : at + t[0].size].reshape(-1, *t.shape[1:])
        gathered.append(jnp.moveaxis(share, 0, dim))
        at += t[0].size
    return tuple(gathered)


def layer_norm(values):
    average = jnp.mean(values, axis=-1, keepdims=True)
    centred = values - average
    spread = jnp.mean(centred * centred, axis=-1, keepdims=True)
    return centred * lax.rsqrt(spread + 1e-05)


def window_attention(normed, qkv_weight, proj_weight, head_count, head_size, window, counts):
    row_count = normed.shape[0]
    window_total = row_count // window
    weight_heads = qkv_weight.reshape(qkv_weight.shape[0], head_count, 3 * head_size)
    packed = jnp.einsum(
        "nc,chj->hnj", normed, weight_heads, preferred_element_type=jnp.float32
    ).astype(jnp.bfloat16)
    packed = packed.reshape(head_count, window_total, window, 3 * head_size)
    queries = packed[..., :head_size]
    key_part = packed[..., head_size : 2 * head_size]
    value_part = packed[..., 2 * head_size :]
    scores = jnp.einsum(
        "hwqd,hwkd->hwqk", queries, key_part, preferred_element_type=jnp.float32
    ) * head_size ** (-0.5)
    if counts is not None:
        position = jnp.arange(window, dtype=jnp.int32)
        visible = position[None, :] < counts[:, None]
        scores = jnp.where(visible[None, :, None, :], scores, -1e30)
    row_max = jnp.max(scores, axis=-1, keepdims=True)
    raised = jnp.exp(scores - row_max)
    weights = (raised / jnp.sum(raised, axis=-1, keepdims=True)).astype(jnp.bfloat16)
    blended = jnp.einsum(
        "hwqk,hwkd->hwqd", weights, value_part, preferred_element_type=jnp.float32
    ).astype(jnp.bfloat16)
    blended = blended.reshape(head_count, row_count, head_size)
    proj_heads = proj_weight.reshape(head_count, head_size, proj_weight.shape[1])
    return jnp.einsum("hnd,hdc->nc", blended, proj_heads, preferred_element_type=jnp.float32)


def hidden_layer(normed, up_weight):
    hidden = jnp.dot(normed, up_weight, preferred_element_type=jnp.float32)
    return jax.nn.gelu(hidden, approximate=False).astype(jnp.bfloat16)


def body(
    fine_tokens,
    fine_shift,
    window_counts,
    fine_qkv,
    fine_proj,
    fine_up,
    fine_down,
    merge_weight,
    coarse_qkv,
    coarse_proj,
    coarse_up,
    coarse_down,
    expand_weight,
    out_weight,
):
    offset = fine_shift[0]
    local_rows = fine_tokens.shape[0]
    normed = layer_norm(fine_tokens).astype(jnp.bfloat16)
    extended = with_halo(normed, ((("region", "head"), 0),), WIN)
    rolled = lax.dynamic_slice_in_dim(extended, offset, local_rows + WIN, 0)
    attended = window_attention(rolled, fine_qkv, fine_proj, HF, HD, WIN, None)
    restored = lax.dynamic_slice_in_dim(attended, WIN - offset, local_rows, 0)
    fine_mid = fine_tokens + restored
    fine_hidden = hidden_layer(layer_norm(fine_mid).astype(jnp.bfloat16), fine_up)
    fine_out = fine_mid + jnp.dot(fine_hidden, fine_down, preferred_element_type=jnp.float32)
    merged = fine_out.reshape(local_rows // 4, 4 * C)
    grouped = layer_norm(merged).astype(jnp.bfloat16)
    coarse = jnp.dot(grouped, merge_weight, preferred_element_type=jnp.float32)
    coarse_norm = layer_norm(coarse).astype(jnp.bfloat16)
    weight_parts = (coarse_qkv, coarse_proj, coarse_up, coarse_down)
    columns = (
        gathered_copies(weight_parts[0], "head", 1),
        gathered_copies(weight_parts[1], "head", 0),
        gathered_copies(weight_parts[2], "head", 1),
        gathered_copies(weight_parts[3], "head", 0),
    )
    qkv_full, proj_full, up_full, down_full = turned_gather(
        (columns[0], columns[1], columns[2], columns[3]), "region", (0, 1, 0, 1)
    )
    window_total = coarse_norm.shape[0] // WIN
    own_counts = lax.dynamic_slice_in_dim(
        window_counts, lax.axis_index("head") * window_total, window_total, 0
    )
    coarse_mid = coarse + window_attention(
        coarse_norm, qkv_full, proj_full, HC, HD, WIN, own_counts
    )
    coarse_hidden = hidden_layer(layer_norm(coarse_mid).astype(jnp.bfloat16), up_full)
    coarse_out = coarse_mid + jnp.dot(coarse_hidden, down_full, preferred_element_type=jnp.float32)
    expanded = jnp.dot(
        coarse_out.astype(jnp.bfloat16), expand_weight, preferred_element_type=jnp.float32
    ).astype(jnp.bfloat16)
    spread_rows = expanded.reshape(local_rows, C)
    joined = jnp.concatenate([fine_out.astype(jnp.bfloat16), spread_rows], axis=1)
    return jnp.dot(joined, out_weight, preferred_element_type=jnp.float32)


def solution(mesh):
    in_specs = (
        P(("region", "head"), None),
        P(),
        P("region"),
        P(),
        P(),
        P(),
        P(),
        P(),
        P("region", "head"),
        P("head", "region"),
        P("region", "head"),
        P("head", "region"),
        P(),
        P(),
    )
    out_specs = P(("region", "head"), None)
    return jax.shard_map(body, mesh=mesh, in_specs=in_specs, out_specs=out_specs, check_vma=False)
```

profile of v0, /device:TPU:23, one launch (start us, length us, event | category | flops | bytes accessed | tf_op | source)
XLA Modules:
  0.0 256.5 jit_solution(4802875899977580490)
XLA Ops:
  6.5 0.9 broadcast_in_dim.18
  7.4 9.6 %all_to_all.20 = bf16[8,128,64]{1,2,0:T(8,128)(2,1)} all-to-all(bf16[8,128,64]{1,2,0:T(8,128)(2,1)S(1)} %broadcast_in_dim.18), channel_id=1, replica_groups=mesh['region'=16,'head'=8] {'head'}, dimensions={0} | all-to-all | bytes 262144 | tf_op jit(solution)/shard_map/all_to_all | solution.py:35
  17.0 0.8 broadcast_in_dim.17
  17.8 10.8 %all_to_all.21 = bf16[8,64,384]{2,1,0:T(8,128)(2,1)S(1)} all-to-all(bf16[8,64,384]{2,1,0:T(8,128)(2,1)S(1)} %broadcast_in_dim.17), channel_id=1, replica_groups=mesh['region'=16,'head'=8] {'head'}, dimensions={0} | all-to-all | bytes 786432 | tf_op jit(solution)/shard_map/all_to_all | solution.py:35
  28.6 0.9 broadcast_in_dim.20
  29.5 12.0 %all_to_all.22 = bf16[8,512,64]{1,2,0:T(8,128)(2,1)S(1)} all-to-all(bf16[8,512,64]{1,2,0:T(8,128)(2,1)S(1)} %broadcast_in_dim.20), channel_id=1, replica_groups=mesh['region'=16,'head'=8] {'head'}, dimensions={0} | all-to-all | bytes 1048576 | tf_op jit(solution)/shard_map/all_to_all | solution.py:35
  41.5 0.8 broadcast_in_dim.19
  42.3 7.1 %all-to-all-start.2 = ((bf16[8,64,512]{2,1,0:T(8,128)(2,1)}), bf16[8,64,512]{2,1,0:T(8,128)(2,1)S(1)}, u32[]{:S(2)}, u32[]{:S(2)}) async-start(bf16[8,64,512]{2,1,0:T(8,128)(2,1)} %broadcast_in_dim.19), calls=%async_computation.2 | async-start | bytes 1048576 | tf_op jit(solution)/shard_map/all_to_all | solution.py:35
  49.4 1.6 bitcast_bitcast_fusion
  51.0 0.8 copy.81
  51.8 0.8 copy.84
  52.7 1.9 all-to-all-done.2
  54.6 0.0 copy-start.2
  54.6 2.5 pad_maximum_fusion
  57.2 0.0 all-gather.2.cloned.1.call-update
  57.2 0.0 copy-start.9
  57.2 0.2 reduce_sum.122
  57.4 0.3 multiply_reduce_fusion.3
  57.7 0.2 multiply_convert_fusion.2
  57.9 0.0 copy-start.6
  57.9 0.8 copy-done.6
  58.7 0.7 fusion.181
  59.4 10.6 %collective-permute-start = (bf16[144,512]{1,0:T(8,128)(2,1)}, bf16[144,512]{1,0:T(8,128)(2,1)}, u32[]{:S(2)}, u32[]{:S(2)}) collective-permute-start(bf16[144,512]{1,0:T(8,128)(2,1)} %get-tuple-element.10), channel_id=1, source_target_pairs={{0,1},{1,2},{2,3},{3,4},{4,5},{5,6},{6,7},{7,8},{8,9},{9,10},{10,1... | collective-permute-start | bytes 442376 | tf_op jit(solution)/shard_map/ppermute | solution.py:21
  70.0 0.0 collective-permute-start.1
  70.7 0.6 dynamic_slice.11
  71.3 0.6 iota_compare_fusion
  72.0 0.5 collective-permute-done
  72.5 6.9 %collective-permute-done.1 = bf16[144,512]{1,0:T(8,128)(2,1)} collective-permute-done((bf16[144,512]{1,0:T(8,128)(2,1)S(1)}, bf16[144,512]{1,0:T(8,128)(2,1)}, u32[]{:S(2)}, u32[]{:S(2)}) %collective-permute-start.1) | collective-permute-done | bytes 147488 | tf_op jit(solution)/shard_map/ppermute | solution.py:22
  79.3 3.3 %fusion.94 = f32[720,1536]{0,1:S(1)} fusion(bf16[512,1536]{1,0:T(8,128)(2,1)} %param.17, s32[]{:T(128)S(6)} %select_n.14, bf16[144,512]{1,0:T(8,128)(2,1)} %collective-permute-done, bf16[576,512]{1,0:T(8,128)(2,1)} %copy-done.6, bf16[144,512]{1,0:T(8,128)(2,1)} %collective-permute-done.1), kind=kOutput, calls=%fused_computation.122 | convolution fusion | flops 1134673920 | bytes 7176196
  82.6 1.7 convert_bitcast_fusion
  84.4 4.5 %copy.55 = bf16[8,720,192]{2,1,0:T(8,128)(2,1)} copy(bf16[8,720,192]{1,2,0:T(8,128)(2,1)} %convert_bitcast_fusion) | data formatting | bytes 4423680 | tf_op jit(solution)/shard_map/convert_element_type | solution.py:75
  88.9 2.9 %fusion.35 = f32[8,5,144,144]{2,3,1,0:T(8,128)S(1)} fusion(bf16[8,5,144,192]{3,2,1,0:T(8,128)(2,1)} %bitcast.89), kind=kOutput, calls=%fused_computation.61 | convolution fusion | flops 106168320 | bytes 5529600 | tf_op jit(solution)/shard_map/hwqd,hwkd->hwqk/dot_general | solution.py:80
  91.8 5.6 %fusion.182 = (f32[8,5,144]{2,1,0:T(8,128)S(1)}, f32[8,5,144,144]{2,3,1,0:T(8,128)S(1)}) fusion(f32[8,5,144,144]{2,3,1,0:T(8,128)S(1)} %fusion.35), kind=kOutput, calls=%fused_computation.223 | output fusion | flops 3317903 | bytes 6658560 | tf_op jit(solution)/shard_map/sub | solution.py:88
  97.5 1.9 fusion.34
  99.4 2.7 %copy.60 = bf16[8,5,144,64]{3,2,1,0:T(8,128)(2,1)} copy(bf16[8,5,144,64]{2,3,1,0:T(8,128)(2,1)} %fusion.34) | data formatting | bytes 1474560 | tf_op jit(solution)/shard_map/convert_element_type | solution.py:92
  102.0 2.2 convolution_bitcast_fusion
  104.3 0.3 fusion.179
  104.6 1.0 copy-done.4
  105.6 0.3 multiply_reduce_fusion.2
  105.9 14.3 %fusion.183 = (f32[576]{0:T(1024)S(1)}, f32[576,512]{1,0:T(8,128)S(1)}) fusion(f32[576,512]{1,0:T(8,128)} %copy-done.4, bf16[2048,512]{1,0:T(8,128)(2,1)S(1)} %copy-done, bf16[512,2048]{1,0:T(8,128)(2,1)} %param.19, f32[576]{0:T(1024)S(1)} %add_rsqrt_fusion, f32[576]{0:T(1024)S(1)} %broadcast_multiply_fusion), kind=kOutput, calls=%fused_computation.224 | convolution fusion | flops 2494070272 | bytes 6560512 | tf_op jit(solution)/shard_map/dot_general | solution.py:128
  120.2 0.1 reduce_sum.128
  120.3 0.1 reduce_sum.129
  120.4 0.1 sub.78
  120.5 0.1 sub.79
  120.6 0.5 reshape.155
  121.2 1.1 fusion.180
  122.3 0.1 reduce_sum.131
  122.4 0.1 reduce_sum.132
  122.5 3.3 %fusion.184 = (f32[144]{0:T(256)S(1)}, f32[144,1024]{1,0:T(8,128)S(1)}) fusion(bf16[2048,1024]{1,0:T(8,128)(2,1)} %param.21, f32[144,2048]{1,0:T(8,128)S(1)} %reshape.155, f32[144]{0:T(256)S(1)} %add_rsqrt_fusion.4, f32[144]{0:T(256)S(1)} %broadcast_multiply_fusion.4), kind=kOutput, calls=%fused_computation.225 | convolution fusion | flops 605011840 | bytes 5965504 | tf_op jit(solution)/shard_map/dot_general | solution.py:131
  125.8 0.2 multiply_reduce_fusion.5
  126.0 71.1 %all-gather.2.cloned.1.call-done = bf16[1024,12288]{1,0:T(8,128)(2,1)} async-done(((bf16[64,12288]{1,0:T(8,128)(2,1)}), bf16[1024,12288]{1,0:T(8,128)(2,1)}) %all-gather.2.cloned.1.call-update) | async-done | bytes 25165840 | tf_op jit(solution)/shard_map/all_gather | solution.py:54
  197.2 5.9 %slice.53 = bf16[1024,3072]{1,0:T(8,128)(2,1)} slice(bf16[1024,12288]{1,0:T(8,128)(2,1)} %all-gather.2.cloned.1.call-done), slice={[0:1024], [0:3072]} | slice | bytes 12582912 | tf_op jit(solution)/shard_map/slice | solution.py:56
  203.1 8.6 %copy.66 = bf16[1024,3072]{0,1:T(8,128)(2,1)} copy(bf16[1024,3072]{1,0:T(8,128)(2,1)} %slice.53) | data formatting | bytes 12582912 | tf_op jit(solution)/shard_map/slice | solution.py:56
  211.7 1.8 slice_bitcast_fusion
  213.5 2.6 %copy.71 = bf16[1024,1024]{1,0:T(8,128)(2,1)} copy(bf16[1024,1024]{0,1:T(8,128)(2,1)S(1)} %slice_bitcast_fusion) | data formatting | bytes 4194304 | tf_op jit(solution)/shard_map/transpose | solution.py:57
  216.0 6.2 %fusion.39 = bf16[16,1,144,192]{3,2,0,1:T(8,128)(2,1)} fusion(bf16[1024,16,192]{0,2,1:T(8,128)(2,1)} %bitcast.91, f32[144,1024]{1,0:T(8,128)S(1)} %get-tuple-element.16, f32[144]{0:T(256)S(1)} %add_rsqrt_fusion.3, f32[144]{0:T(256)S(1)} %broadcast_multiply_fusion.3), kind=kOutput, calls=%fused_computation.66 | convolution fusion | flops 906854400 | bytes 7767168 | tf_op jit(solution)/shard_map/nc,chj->hnj/dot_general | solution.py:73
  222.2 3.8 %fusion.185 = (f32[16,144]{1,0:T(8,128)S(1)}, f32[16,144,144]{1,2,0:T(8,128)}) fusion(pred[144]{0:T(512)(128)(4,1)S(1)} %iota_compare_fusion, bf16[16,1,144,192]{3,2,0,1:T(8,128)(2,1)} %fusion.39), kind=kOutput, calls=%fused_computation.226 | convolution fusion | flops 43794576 | bytes 2221200 | tf_op jit(solution)/shard_map/sub | solution.py:88
  226.1 2.7 %fusion.186 = (f32[144]{0:T(256)S(1)}, f32[144,1024]{1,0:T(8,128)S(1)}) fusion(f32[144,1024]{1,0:T(8,128)S(1)} %get-tuple-element.16, bf16[16,64,1024]{2,1,0:T(8,128)(2,1)S(1)} %bitcast.93, f32[16,144,144]{1,2,0:T(8,128)} %get-tuple-element.18, f32[16,144]{1,0:T(8,128)S(1)} %get-tuple-element.17, bf16[16,1,144,192]{3,2,0,1:T(8,128)(2,1)} %fusion.39), kind=kOutput, calls=%fused_computation.227 | convolution fusion | flops 345563008 | bytes 6235712 | tf_op jit(solution)/shard_map/hnd,hdc->nc/dot_general | solution.py:95
  228.7 0.2 multiply_reduce_fusion.4
  229.0 13.2 %fusion.47 = bf16[144,1024]{1,0:T(8,128)(2,1)S(1)} fusion(f32[144,1024]{1,0:T(8,128)S(1)} %get-tuple-element.20, bf16[1024,12288]{1,0:T(8,128)(2,1)} %all-gather.2.cloned.1.call-done, f32[144]{0:T(256)S(1)} %add_rsqrt_fusion.2, f32[144]{0:T(256)S(1)} %broadcast_multiply_fusion.2), kind=kOutput, calls=%fused_computation.72 | convolution fusion | flops 2454994944 | bytes 18253824 | tf_op jit(solution)/shard_map/dot_general | solution.py:151
  242.2 3.0 %convolution_convert_fusion = bf16[144,2048]{1,0:T(8,128)(2,1)S(1)} fusion(bf16[144,1024]{1,0:T(8,128)(2,1)S(1)} %fusion.47, bf16[1024,2048]{1,0:T(8,128)(2,1)} %param.26), kind=kOutput, calls=%fused_computation.32 | convolution fusion | flops 604274688 | bytes 5079040 | tf_op jit(solution)/shard_map/dot_general | solution.py:152
  245.3 0.0 copy-start.1
  245.3 1.2 reshape.166
  246.4 3.2 %fusion.55 = f32[576,512]{1,0:T(8,128)} fusion(bf16[1024,512]{1,0:T(8,128)(2,1)} %param.27, bf16[576,512]{1,0:T(8,128)(2,1)} %reshape.166, bf16[576,512]{1,0:T(8,128)(2,1)S(1)} %copy-done.7), kind=kOutput, calls=%fused_computation.73 | convolution fusion | flops 606339072 | bytes 3407872 | tf_op jit(solution)/shard_map/dot_general | solution.py:157
  (26 shorter events, 0.1 us)
Async XLA Ops:
  6.5 99.4 %copy-start = (bf16[2048,512]{1,0:T(8,128)(2,1)S(1)}, bf16[2048,512]{1,0:T(8,128)(2,1)}, u32[]{:S(2)}) copy-start(bf16[2048,512]{1,0:T(8,128)(2,1)} %param.20) | copy-start | bytes 6291460
  6.5 34.9 %copy-start.8 = (bf16[64,512]{1,0:T(8,128)(2,1)S(1)}, bf16[64,512]{1,0:T(8,128)(2,1)}, u32[]{:S(2)}) copy-start(bf16[64,512]{1,0:T(8,128)(2,1)} %param.24) | copy-start | bytes 196612
  42.3 12.3 %all-to-all-start.2 = ((bf16[8,64,512]{2,1,0:T(8,128)(2,1)}), bf16[8,64,512]{2,1,0:T(8,128)(2,1)S(1)}, u32[]{:S(2)}, u32[]{:S(2)}) async-start(bf16[8,64,512]{2,1,0:T(8,128)(2,1)} %broadcast_in_dim.19), calls=%async_computation.2 | async-start | bytes 1048576 | tf_op jit(solution)/shard_map/all_to_all | solution.py:35
  49.4 147.7 %all-gather.2.cloned.1.call-start = ((), (), s32[]{:S(2)}) async-start(), calls=%async_computation.4 | async-start | bytes 26738688 | tf_op jit(solution)/shard_map/all_gather | solution.py:54
  54.6 2.6 %copy-start.2 = (f32[576,512]{1,0:T(8,128)S(1)}, f32[576,512]{1,0:T(8,128)}, u32[]{:S(2)}) copy-start(f32[576,512]{1,0:T(8,128)} %param.14) | copy-start | bytes 3538948
  57.2 13.5 %copy-start.9 = (s32[8]{0:T(128)S(1)}, s32[8]{0:T(128)}, u32[]{:S(2)}) copy-start(s32[8]{0:T(128)} %param.16) | copy-start | bytes 100
  57.9 0.8 copy-start.6
  59.4 13.0 %collective-permute-start = (bf16[144,512]{1,0:T(8,128)(2,1)}, bf16[144,512]{1,0:T(8,128)(2,1)}, u32[]{:S(2)}, u32[]{:S(2)}) collective-permute-start(bf16[144,512]{1,0:T(8,128)(2,1)} %get-tuple-element.10), channel_id=1, source_target_pairs={{0,1},{1,2},{2,3},{3,4},{4,5},{5,6},{6,7},{7,8},{8,9},{9,10},{10,1... | collective-permute-start | bytes 442376 | tf_op jit(solution)/shard_map/ppermute | solution.py:21
  70.0 9.3 %collective-permute-start.1 = (bf16[144,512]{1,0:T(8,128)(2,1)S(1)}, bf16[144,512]{1,0:T(8,128)(2,1)}, u32[]{:S(2)}, u32[]{:S(2)}) collective-permute-start(bf16[144,512]{1,0:T(8,128)(2,1)S(1)} %get-tuple-element.9), channel_id=1, source_target_pairs={{1,0},{2,1},{3,2},{4,3},{5,4},{6,5},{7,6},{8,7},{9,8},{10,9},{11,1... | collective-permute-start | bytes 442376 | tf_op jit(solution)/shard_map/ppermute | solution.py:22
  91.8 5.6 %copy-start.3 = (bf16[8,720,192]{2,1,0:T(8,128)(2,1)S(1)}, bf16[8,720,192]{2,1,0:T(8,128)(2,1)}, u32[]{:S(2)}) copy-start(bf16[8,720,192]{2,1,0:T(8,128)(2,1)} %copy.55) | copy-start | bytes 6635524
  104.6 1.0 copy-start.4
  222.2 3.8 %copy-start.5 = (bf16[1024,1024]{1,0:T(8,128)(2,1)S(1)}, bf16[1024,1024]{1,0:T(8,128)(2,1)}, u32[]{:S(2)}) copy-start(bf16[1024,1024]{1,0:T(8,128)(2,1)} %copy.71) | copy-start | bytes 6291460
  242.2 4.2 %copy-start.7 = (bf16[576,512]{1,0:T(8,128)(2,1)S(1)}, bf16[576,512]{1,0:T(8,128)(2,1)}, u32[]{:S(2)}) copy-start(bf16[576,512]{1,0:T(8,128)(2,1)} %get-tuple-element.7) | copy-start | bytes 1769476
  245.3 4.4 %copy-start.1 = (bf16[2048,512]{1,0:T(8,128)(2,1)S(1)}, bf16[2048,512]{1,0:T(8,128)(2,1)}, u32[]{:S(2)}) copy-start(bf16[2048,512]{1,0:T(8,128)(2,1)} %param.20) | copy-start | bytes 6291460
Sparse Core Ops, SparseCore 0:
  57.3 139.8 all-gather.1
where the time goes:
time: 258 us; the launch traced here: 256 us
  waiting for transfers between devices  80.4 us (31%)
  matrix products  60.1 us (23%)
  local copies, waits for them, and re-layouts  38 us (15%)
  blocking collectives  32.3 us (13%)
  starting transfers between devices  17.8 us (7%)
  between operations  14.3 us (6%)
  other arithmetic  13.6 us (5%)
    all_gather x1, waiting for transfers between devices, turned_gather(): lax.all_gather(both, axis, axis=0, tiled=True)  71.1 us
    all_to_all x3, blocking collectives, from_everyone(): lax.all_to_all(jnp.broadcast_to(value[None], (devices, *value.shape)), ax...  32.3 us
    slice x2, local copies, waits for them, and re-layouts, turned_gather(): share = filled[:, at:at + t[0].size].reshape(-1, *t.shape[1:])  14.5 us
    dot_general x1, matrix products, body(): jnp.dot(fine_hidden, fine_down, preferred_element_type=jnp.float32)  14.3 us
    dot_general x1, matrix products, body(): jnp.dot(coarse_hidden, down_full, preferred_element_type=jnp.float32)  13.2 us
    ppermute x1, starting transfers between devices, with_halo(): lax.ppermute(last, axis, up)  10.6 us
    all_to_all x1, starting transfers between devices, from_everyone(): lax.all_to_all(jnp.broadcast_to(value[None], (devices, *value.shape)), ax...  7.13 us
    ppermute x1, waiting for transfers between devices, with_halo(): lax.ppermute(initial, axis, [(b, a) for a, b in up])  6.87 us
  transfers between devices with their start and end apart: 4, of which 4 were waited for; matrix products, arithmetic and copies ran while one was open for 20% of the time, Pallas kernels for 0%

commit v1 on v0

--- a/solution.py
+++ b/solution.py
@@ -51,7 +51,19 @@
 def turned_gather(arrays, axis, dims):
     turned = [jnp.moveaxis(a, dim, 0) for a, dim in zip(arrays, dims)]
     both = jnp.concatenate([t.reshape(len(t), -1) for t in turned], axis=1)
-    filled, at, gathered = (lax.all_gather(both, axis, axis=0, tiled=True), 0, [])
+    filled, at, gathered = (
+        jnp.concatenate(
+            jax.lax.all_to_all(
+                jnp.stack([both for _ in range(jax.lax.psum(1, axis_name=axis))], axis=0),
+                axis,
+                0,
+                0,
+            ),
+            axis=0,
+        ),
+        0,
+        [],
+    )
     for t, dim in zip(turned, dims):
         share = filled[:, at : at + t[0].size].reshape(-1, *t.shape[1:])
         gathered.append(jnp.moveaxis(share, 0, dim))

time: 258 us -> 524 us (2.03); the launches traced: 256 us -> 514 us
  waiting for transfers between devices: 80.4 us -> 339 us
  between operations: 14.3 us -> 0.95 us
  local copies, waits for them, and re-layouts: 38 us -> 46.6 us
  starting transfers between devices: 17.8 us -> 23.4 us
    all_to_all x0 -> x1, waiting for transfers between devices: none -> 329 us  [turned_gather(): jax.lax.all_to_all(jnp.stack([both for _ in range(jax.lax.psum(1, axis_na...]
    all_gather x1 -> x0, waiting for transfers between devices: 71.1 us -> none  [turned_gather(): lax.all_gather(both, axis, axis=0, tiled=True)]
    all_to_all x0 -> x1, starting transfers between devices: none -> 11.6 us  [turned_gather(): jax.lax.all_to_all(jnp.stack([both for _ in range(jax.lax.psum(1, axis_na...]
    another operation x0 -> x1, local copies, waits for them, and re-layouts: none -> 8.58 us  [turned_gather(): jnp.stack([both for _ in range(jax.lax.psum(1, axis_name=axis))], axis=0)]
    ppermute x1, starting transfers between devices: 10.6 us -> 4.66 us  [with_halo(): lax.ppermute(last, axis, up)]
  transfers between devices with their start and end apart: 4 -> 4, of which waited for: 4 -> 4; matrix products, arithmetic and copies ran while one was open for 20% -> 10% of each run, Pallas kernels for 0% -> 0%
where the time goes in v1:
time: 524 us; the launch traced here: 514 us
  waiting for transfers between devices  339 us (65%)
  matrix products  59.5 us (11%)
  local copies, waits for them, and re-layouts  46.6 us (9%)
  blocking collectives  32.3 us (6%)
  starting transfers between devices  23.4 us (4%)
  other arithmetic  12.2 us (2%)
    all_to_all x1, waiting for transfers between devices, turned_gather(): jax.lax.all_to_all(jnp.stack([both for _ in range(jax.lax.psum(1, axis_na...  329 us
    all_to_all x3, blocking collectives, from_everyone(): lax.all_to_all(jnp.broadcast_to(value[None], (devices, *value.shape)), ax...  32.3 us
    slice x2, local copies, waits for them, and re-layouts, turned_gather(): share = filled[:, at:at + t[0].size].reshape(-1, *t.shape[1:])  14.6 us
    dot_general x1, matrix products, body(): jnp.dot(fine_hidden, fine_down, preferred_element_type=jnp.float32)  14.1 us
    dot_general x1, matrix products, body(): jnp.dot(coarse_hidden, down_full, preferred_element_type=jnp.float32)  13.2 us
    all_to_all x1, starting transfers between devices, turned_gather(): jax.lax.all_to_all(jnp.stack([both for _ in range(jax.lax.psum(1, axis_na...  11.6 us
  transfers between devices with their start and end apart: 4, of which 4 were waited for; matrix products, arithmetic and copies ran while one was open for 10% of the time, Pallas kernels for 0%

profile of v1, /device:TPU:23, one launch (start us, length us, event | category | flops | bytes accessed | tf_op | source)
XLA Modules:
  0.0 514.3 jit_solution(17543340797690856212)
XLA Ops:
  0.0 0.9 broadcast_in_dim.18
  0.9 9.6 %all_to_all.25 = bf16[8,128,64]{1,2,0:T(8,128)(2,1)} all-to-all(bf16[8,128,64]{1,2,0:T(8,128)(2,1)S(1)} %broadcast_in_dim.18), channel_id=1, replica_groups=mesh['region'=16,'head'=8] {'head'}, dimensions={0} | all-to-all | bytes 262144 | tf_op jit(solution)/shard_map/all_to_all | solution.py:35
  10.5 0.8 broadcast_in_dim.17
  11.3 10.8 %all_to_all.26 = bf16[8,64,384]{2,1,0:T(8,128)(2,1)S(1)} all-to-all(bf16[8,64,384]{2,1,0:T(8,128)(2,1)S(1)} %broadcast_in_dim.17), channel_id=1, replica_groups=mesh['region'=16,'head'=8] {'head'}, dimensions={0} | all-to-all | bytes 786432 | tf_op jit(solution)/shard_map/all_to_all | solution.py:35
  22.1 0.9 broadcast_in_dim.20
  23.0 12.0 %all_to_all.27 = bf16[8,512,64]{1,2,0:T(8,128)(2,1)S(1)} all-to-all(bf16[8,512,64]{1,2,0:T(8,128)(2,1)S(1)} %broadcast_in_dim.20), channel_id=1, replica_groups=mesh['region'=16,'head'=8] {'head'}, dimensions={0} | all-to-all | bytes 1048576 | tf_op jit(solution)/shard_map/all_to_all | solution.py:35
  34.9 0.8 broadcast_in_dim.19
  35.8 7.1 %all-to-all-start.2 = ((bf16[8,64,512]{2,1,0:T(8,128)(2,1)}), bf16[8,64,512]{2,1,0:T(8,128)(2,1)S(1)}, u32[]{:S(2)}, u32[]{:S(2)}) async-start(bf16[8,64,512]{2,1,0:T(8,128)(2,1)} %broadcast_in_dim.19), calls=%async_computation.2 | async-start | bytes 1048576 | tf_op jit(solution)/shard_map/all_to_all | solution.py:35
  42.9 1.6 bitcast_bitcast_fusion
  44.5 0.8 copy.79
  45.3 0.8 copy.82
  46.1 1.9 all-to-all-done.2
  48.1 1.2 pad_maximum_fusion
  49.2 8.6 %stack.2 = bf16[16,64,12288]{2,1,0:T(8,128)(2,1)} broadcast(bf16[64,12288]{1,0:T(8,128)(2,1)S(1)} %pad_maximum_fusion), dimensions={1,2} | broadcast | bytes 26738688 | tf_op jit(solution)/shard_map/stack | solution.py:57
  57.8 11.6 %all-to-all-start.4 = ((bf16[16,64,12288]{2,1,0:T(8,128)(2,1)}), bf16[16,64,12288]{2,1,0:T(8,128)(2,1)}, u32[]{:S(2)}, u32[]{:S(2)}) async-start(bf16[16,64,12288]{2,1,0:T(8,128)(2,1)} %stack.2), calls=%async_computation.4 | async-start | bytes 50331648 | tf_op jit(solution)/shard_map/all_to_all | solution.py:56
  69.5 0.0 copy-start.10
  69.5 0.2 reduce_sum.122
  69.7 0.3 multiply_reduce_fusion.3
  70.0 0.2 multiply_convert_fusion.2
  70.2 0.0 copy-start.7
  70.2 0.8 copy-done.7
  71.0 0.7 fusion.181
  71.7 4.7 collective-permute-start
  76.4 0.0 collective-permute-start.1
  77.0 0.7 dynamic_slice.11
  77.7 0.7 iota_compare_fusion
  78.4 1.2 collective-permute-done
  79.6 7.4 %collective-permute-done.1 = bf16[144,512]{1,0:T(8,128)(2,1)} collective-permute-done((bf16[144,512]{1,0:T(8,128)(2,1)S(1)}, bf16[144,512]{1,0:T(8,128)(2,1)}, u32[]{:S(2)}, u32[]{:S(2)}) %collective-permute-start.1) | collective-permute-done | bytes 147488 | tf_op jit(solution)/shard_map/ppermute | solution.py:22
  87.0 3.3 fusion.94
  90.2 1.7 convert_bitcast_fusion
  91.9 4.5 copy.53
  96.4 2.9 fusion.35
  99.3 5.6 %fusion.182 = (f32[8,5,144]{2,1,0:T(8,128)S(1)}, f32[8,5,144,144]{2,3,1,0:T(8,128)S(1)}) fusion(f32[8,5,144,144]{2,3,1,0:T(8,128)S(1)} %fusion.35), kind=kOutput, calls=%fused_computation.223 | output fusion | flops 3317903 | bytes 6658560 | tf_op jit(solution)/shard_map/sub | solution.py:100
  105.0 1.9 fusion.34
  106.9 2.7 copy.58
  109.5 2.1 convolution_bitcast_fusion
  111.6 0.3 fusion.179
  111.9 1.0 copy-done.4
  112.9 0.3 multiply_reduce_fusion.2
  113.2 14.1 %fusion.183 = (f32[576]{0:T(1024)S(1)}, f32[576,512]{1,0:T(8,128)S(1)}) fusion(f32[576,512]{1,0:T(8,128)} %copy-done.4, bf16[2048,512]{1,0:T(8,128)(2,1)S(1)} %copy-done, bf16[512,2048]{1,0:T(8,128)(2,1)} %param.19, f32[576]{0:T(1024)S(1)} %add_rsqrt_fusion, f32[576]{0:T(1024)S(1)} %broadcast_multiply_fusion), kind=kOutput, calls=%fused_computation.224 | convolution fusion | flops 2494070272 | bytes 6560512 | tf_op jit(solution)/shard_map/dot_general | solution.py:140
  127.3 0.5 reshape.160
  127.8 0.1 reduce_sum.128
  128.0 0.1 reduce_sum.129
  128.1 0.1 sub.78
  128.2 0.1 sub.79
  128.3 1.1 fusion.180
  129.4 0.1 reduce_sum.131
  129.5 0.1 reduce_sum.132
  129.6 3.1 fusion.184
  132.8 0.2 multiply_reduce_fusion.5
  133.0 328.7 %all-to-all-done.4 = bf16[16,64,12288]{2,1,0:T(8,128)(2,1)} async-done(((bf16[16,64,12288]{2,1,0:T(8,128)(2,1)}), bf16[16,64,12288]{2,1,0:T(8,128)(2,1)}, u32[]{:S(2)}, u32[]{:S(2)}) %all-to-all-start.4) | async-done | bytes 25165856 | tf_op jit(solution)/shard_map/all_to_all | solution.py:56
  461.7 1.8 slice_bitcast_fusion
  463.5 5.9 %slice.53 = bf16[1024,3072]{1,0:T(8,128)(2,1)} slice(bf16[1024,12288]{1,0:T(8,128)(2,1)} %bitcast.14), slice={[0:1024], [0:3072]} | slice | bytes 12582912 | tf_op jit(solution)/shard_map/slice | solution.py:68
  469.4 2.5 copy.69
  472.0 8.7 %copy.64 = bf16[1024,3072]{0,1:T(8,128)(2,1)} copy(bf16[1024,3072]{1,0:T(8,128)(2,1)} %slice.53) | data formatting | bytes 12582912 | tf_op jit(solution)/shard_map/slice | solution.py:68
  480.7 6.2 %fusion.39 = bf16[16,1,144,192]{3,2,0,1:T(8,128)(2,1)} fusion(bf16[1024,16,192]{0,2,1:T(8,128)(2,1)} %bitcast.92, f32[144,1024]{1,0:T(8,128)S(1)} %get-tuple-element.16, f32[144]{0:T(256)S(1)} %add_rsqrt_fusion.3, f32[144]{0:T(256)S(1)} %broadcast_multiply_fusion.3), kind=kOutput, calls=%fused_computation.66 | convolution fusion | flops 906854400 | bytes 7767168 | tf_op jit(solution)/shard_map/nc,chj->hnj/dot_general | solution.py:85
  486.8 3.8 fusion.185
  490.7 2.7 fusion.186
  493.4 0.2 multiply_reduce_fusion.4
  493.6 13.2 %fusion.47 = bf16[144,1024]{1,0:T(8,128)(2,1)S(1)} fusion(f32[144,1024]{1,0:T(8,128)S(1)} %get-tuple-element.20, bf16[1024,12288]{1,0:T(8,128)(2,1)} %bitcast.14, f32[144]{0:T(256)S(1)} %add_rsqrt_fusion.2, f32[144]{0:T(256)S(1)} %broadcast_multiply_fusion.2), kind=kOutput, calls=%fused_computation.72 | convolution fusion | flops 2454994944 | bytes 18253824 | tf_op jit(solution)/shard_map/dot_general | solution.py:163
  506.9 3.0 convolution_convert_fusion
  509.9 0.0 copy-start.1
  509.9 1.2 reshape.172
  511.1 3.2 fusion.55
  (28 shorter events, 0.1 us)
Async XLA Ops:
  0.0 113.2 %copy-start = (bf16[2048,512]{1,0:T(8,128)(2,1)S(1)}, bf16[2048,512]{1,0:T(8,128)(2,1)}, u32[]{:S(2)}) copy-start(bf16[2048,512]{1,0:T(8,128)(2,1)} %param.20) | copy-start | bytes 6291460
  0.0 34.9 %copy-start.9 = (bf16[64,512]{1,0:T(8,128)(2,1)S(1)}, bf16[64,512]{1,0:T(8,128)(2,1)}, u32[]{:S(2)}) copy-start(bf16[64,512]{1,0:T(8,128)(2,1)} %param.24) | copy-start | bytes 196612
  35.8 12.3 %all-to-all-start.2 = ((bf16[8,64,512]{2,1,0:T(8,128)(2,1)}), bf16[8,64,512]{2,1,0:T(8,128)(2,1)S(1)}, u32[]{:S(2)}, u32[]{:S(2)}) async-start(bf16[8,64,512]{2,1,0:T(8,128)(2,1)} %broadcast_in_dim.19), calls=%async_computation.2 | async-start | bytes 1048576 | tf_op jit(solution)/shard_map/all_to_all | solution.py:35
  45.3 2.8 copy-start.6
  57.8 11.6 %copy-start.2 = (f32[576,512]{1,0:T(8,128)S(1)}, f32[576,512]{1,0:T(8,128)}, u32[]{:S(2)}) copy-start(f32[576,512]{1,0:T(8,128)} %param.14) | copy-start | bytes 3538948
  57.8 403.9 %all-to-all-start.4 = ((bf16[16,64,12288]{2,1,0:T(8,128)(2,1)}), bf16[16,64,12288]{2,1,0:T(8,128)(2,1)}, u32[]{:S(2)}, u32[]{:S(2)}) async-start(bf16[16,64,12288]{2,1,0:T(8,128)(2,1)} %stack.2), calls=%async_computation.4 | async-start | bytes 50331648 | tf_op jit(solution)/shard_map/all_to_all | solution.py:56
  69.5 7.5 %copy-start.10 = (s32[8]{0:T(128)S(1)}, s32[8]{0:T(128)}, u32[]{:S(2)}) copy-start(s32[8]{0:T(128)} %param.16) | copy-start | bytes 100
  70.2 0.8 copy-start.7
  71.7 7.9 %collective-permute-start = (bf16[144,512]{1,0:T(8,128)(2,1)}, bf16[144,512]{1,0:T(8,128)(2,1)}, u32[]{:S(2)}, u32[]{:S(2)}) collective-permute-start(bf16[144,512]{1,0:T(8,128)(2,1)} %get-tuple-element.10), channel_id=1, source_target_pairs={{0,1},{1,2},{2,3},{3,4},{4,5},{5,6},{6,7},{7,8},{8,9},{9,10},{10,1... | collective-permute-start | bytes 442376 | tf_op jit(solution)/shard_map/ppermute | solution.py:21
  76.4 10.6 %collective-permute-start.1 = (bf16[144,512]{1,0:T(8,128)(2,1)S(1)}, bf16[144,512]{1,0:T(8,128)(2,1)}, u32[]{:S(2)}, u32[]{:S(2)}) collective-permute-start(bf16[144,512]{1,0:T(8,128)(2,1)S(1)} %get-tuple-element.9), channel_id=1, source_target_pairs={{1,0},{2,1},{3,2},{4,3},{5,4},{6,5},{7,6},{8,7},{9,8},{10,9},{11,1... | collective-permute-start | bytes 442376 | tf_op jit(solution)/shard_map/ppermute | solution.py:22
  99.3 5.6 %copy-start.3 = (bf16[8,720,192]{2,1,0:T(8,128)(2,1)S(1)}, bf16[8,720,192]{2,1,0:T(8,128)(2,1)}, u32[]{:S(2)}) copy-start(bf16[8,720,192]{2,1,0:T(8,128)(2,1)} %copy.53) | copy-start | bytes 6635524
  111.9 1.0 copy-start.4
  486.8 3.8 copy-start.5
  506.8 4.2 copy-start.8
  509.9 4.4 copy-start.1
